TPU v7x, 256 devices: a whole 4x4x8 slice. The times are simulated.
256 devices in a mesh: slab: 32 (over x_hi, z, core), view: 8 (over x_lo, y).
Axes of the slice: x: 4 (x_hi: 2, x_lo: 2; x = x_hi * 2 + x_lo), y: 4, z: 8, core: 2. Of those that a mesh axis runs over, the one named last changes fastest.
Arguments:
- fine_volume: float32 [128, 4096], P('slab'), may hold values from 0 to 1
- coarse_volume: float32 [512, 4096], P('slab'), may hold values from 0 to 1
- fine_rays: bfloat16 [16, 4096, 128], P('view'), may hold values from -0.09375 to 0.09375
- coarse_rays: bfloat16 [16, 4096, 128], P('view'), may hold values from -0.09375 to 0.09375
- fine_axial: bfloat16 [16, 128, 256], P('view', 'slab'), may hold values from -0.3125 to 0.3125
- coarse_axial: bfloat16 [16, 512, 256], P('view', 'slab'), may hold values from -0.21875 to 0.21875
- measured: float32 [256, 16, 128], P('slab', 'view'), may hold values from 0 to 2
- ray_weight: float32 [256, 16, 128], P('slab', 'view'), may hold values from 0.25 to 0.5
- fine_cell_weight: float32 [128, 4096], P('slab'), may hold values from 0.3 to 0.6
- coarse_cell_weight: float32 [512, 4096], P('slab'), may hold values from 0.3 to 0.6
- margin_blocks: int32 [32, 8], P('slab'), may hold values from 0 to 31, as said below
- ray_hits: int32 [16, 32, 8], P('view', 'slab'), may hold values 0 or 1
Outputs:
- fine_result: float32 [128, 4096], P('slab')
- coarse_result: float32 [512, 4096], P('slab')
Inputs may be any that keep to these rules, and one draw needn't show every extreme that they name: `margin_blocks`: each row lists 8 different block numbers.
All inputs are finite; a program needn't handle non-finite values. No bound on the sum of `ray_hits` on one device may be relied on, other than what follows from the above.
Results may differ from a plain program's by a relative error of at most 0.005.
Values may be sent and summed in bfloat16 or wider, within the bound.
A program may use at most 64 MiB of HBM per device.

v0:
```python
import jax
import jax.numpy as jnp
from jax import lax
from jax.sharding import PartitionSpec as P

ITERS = 3
BLOCK = 128


def body(
    fine_volume,
    coarse_volume,
    fine_rays,
    coarse_rays,
    fine_axial,
    coarse_axial,
    measured,
    ray_weight,
    fine_cell_weight,
    coarse_cell_weight,
    margin_blocks,
    ray_hits,
):
    view_count = fine_rays.shape[0]
    detector_rows = fine_axial.shape[2]
    tile_count = ray_hits.shape[2]
    coarse_cells = coarse_volume.shape[1]
    block_ids = jnp.arange(coarse_cells, dtype=jnp.int32) // BLOCK
    listed = jnp.any(margin_blocks[0][:, None] == block_ids[None, :], axis=0)
    keep_mask = jnp.where(listed, 0.0, 1.0).astype(jnp.float32)[None, :]
    hit_rows = jnp.broadcast_to(
        ray_hits[:, 0, :, None], (view_count, tile_count, detector_rows // tile_count)
    )
    hit_rows = hit_rows.reshape(view_count, detector_rows).astype(jnp.bfloat16)
    fine_depth = fine_axial * hit_rows[:, None, :]
    coarse_depth = coarse_axial * hit_rows[:, None, :]
    fine = fine_volume
    coarse = coarse_volume * keep_mask
    whole_measured, whole_weight = (
        lax.all_gather(measured, "slab", axis=0, tiled=True),
        lax.all_gather(ray_weight, "slab", axis=0, tiled=True),
    )
    for iteration in range(ITERS):
        fine_moment = jnp.einsum(
            "zx,vxu->vzu", fine.astype(jnp.bfloat16), fine_rays, preferred_element_type=jnp.float32
        ).astype(jnp.bfloat16)
        coarse_moment = jnp.einsum(
            "zx,vxu->vzu",
            coarse.astype(jnp.bfloat16),
            coarse_rays,
            preferred_element_type=jnp.float32,
        ).astype(jnp.bfloat16)
        total = jnp.einsum(
            "vzw,vzu->wvu", fine_depth, fine_moment, preferred_element_type=jnp.float32
        )
        projection = lax.psum(
            (
                total
                + jnp.einsum(
                    "vzw,vzu->wvu", coarse_depth, coarse_moment, preferred_element_type=jnp.float32
                )
            ).astype(jnp.bfloat16),
            "slab",
        ).astype(jnp.float32)
        residual = (whole_weight * (whole_measured - projection)).astype(jnp.bfloat16)
        fine_spread = jnp.einsum(
            "vzw,wvu->vzu", fine_depth, residual, preferred_element_type=jnp.float32
        ).astype(jnp.bfloat16)
        coarse_spread = jnp.einsum(
            "vzw,wvu->vzu", coarse_depth, residual, preferred_element_type=jnp.float32
        ).astype(jnp.bfloat16)
        fine_term = jnp.einsum(
            "vzu,vxu->zx", fine_spread, fine_rays, preferred_element_type=jnp.float32
        )
        coarse_term = jnp.einsum(
            "vzu,vxu->zx", coarse_spread, coarse_rays, preferred_element_type=jnp.float32
        )
        fine_back, coarse_back = (
            lax.psum(fine_term.astype(jnp.bfloat16), "view").astype(jnp.float32),
            lax.psum(coarse_term.astype(jnp.bfloat16), "view").astype(jnp.float32),
        )
        fine = fine + fine_cell_weight * fine_back
        coarse = (coarse + coarse_cell_weight * coarse_back) * keep_mask
    return (fine, coarse)


def solution(mesh):
    return jax.shard_map(
        body,
        mesh=mesh,
        in_specs=(
            P("slab", None),
            P("slab", None),
            P("view", None, None),
            P("view", None, None),
            P("view", "slab", None),
            P("view", "slab", None),
            P("slab", "view", None),
            P("slab", "view", None),
            P("slab", None),
            P("slab", None),
            P("slab", None),
            P("view", "slab", None),
        ),
        out_specs=(P("slab", None), P("slab", None)),
        check_vma=False,
    )
```

profile of v0, /device:TPU:4, one launch (start us, length us, event | category | flops | bytes accessed | tf_op | source)
XLA Modules:
  0.0 1104.9 jit_solution(4138401398298017130)
XLA Ops:
  7.2 0.0 copy-start
  7.2 0.0 all-reduce.7.cloned.1.call-start
  7.3 0.8 convert_element_type.156
  8.1 0.1 broadcast_in_dim.10
  8.2 0.1 convert_element_type.158
  8.3 0.8 compare_reduce_fusion
  9.1 0.0 copy-start.19
  9.1 2.3 fusion.15
  11.4 0.0 copy-done
  11.4 0.0 copy-done.6
  11.4 0.0 copy-done.1
  11.4 0.0 copy-start.20
  11.4 0.0 copy-start.17
  11.4 1.3 fusion.11
  12.8 0.0 all-reduce.7.cloned.1.call-update
  12.8 0.0 all-reduce.9.cloned.1.call-start
  12.8 42.9 %all_gather.7 = f32[256,2,128]{2,1,0:T(2,128)S(1)} all-gather(f32[8,2,128]{2,1,0:T(2,128)S(1)} %copy-done.19), channel_id=1, replica_groups=mesh['slab'=32,'view'=8] {'slab'}, dimensions={0}, use_global_device_ids=true | all-gather | bytes 270336 | tf_op jit(solution)/shard_map/all_gather | solution.py:40
  55.7 0.1 copy.22
  55.9 0.0 copy-done.20
  55.9 37.4 %all_gather.6 = f32[256,2,128]{2,1,0:T(2,128)S(1)} all-gather(f32[8,2,128]{2,1,0:T(2,128)S(1)} %copy-done.20), channel_id=1, replica_groups=mesh['slab'=32,'view'=8] {'slab'}, dimensions={0}, use_global_device_ids=true | all-gather | bytes 270336 | tf_op jit(solution)/shard_map/all_gather | solution.py:41
  93.3 0.1 copy.23
  93.4 168.4 %all-reduce.7.cloned.1.call-done = bf16[256,2,128]{0,2,1:T(8,128)(2,1)} async-done(((bf16[256,2,128]{0,2,1:T(8,128)(2,1)}), bf16[256,2,128]{0,2,1:T(8,128)(2,1)}) %all-reduce.7.cloned.1.call-update) | async-done | bytes 131088 | tf_op jit(solution)/shard_map/psum | solution.py:56
  261.8 0.9 multiply_convert_fusion.2
  262.8 0.0 copy-done.17
  262.8 0.0 copy-start.4
  262.8 0.0 copy-start.7
  262.8 2.4 fusion.3
  265.1 0.0 copy-done.14
  265.2 1.4 fusion
  266.6 35.3 %psum.64 = bf16[4,4096]{1,0:T(4,128)(2,1)} all-reduce(bf16[4,4096]{1,0:T(4,128)(2,1)S(1)} %fusion.3), channel_id=1, replica_groups=mesh['slab'=32,'view'=8] {'view'}, use_global_device_ids=true, to_apply=%region_2.3 | all-reduce | flops 16384 | bytes 65536 | tf_op jit(solution)/shard_map/psum | solution.py:79
  301.9 0.0 all-reduce.9.cloned.1.call-update
  301.9 0.0 all-reduce.11.cloned.1.call-start
  302.0 2.3 fusion.17
  304.3 0.0 copy-start.18
  304.3 70.4 %all-reduce.9.cloned.1.call-done = bf16[16,4096]{1,0:T(8,128)(2,1)} async-done(((bf16[16,4096]{1,0:T(8,128)(2,1)}), bf16[16,4096]{1,0:T(8,128)(2,1)}) %all-reduce.9.cloned.1.call-update) | async-done | bytes 131088 | tf_op jit(solution)/shard_map/psum | solution.py:80
  374.7 2.2 fusion.10
  376.9 0.0 all-reduce.11.cloned.1.call-update
  376.9 0.0 all-reduce.13.cloned.1.call-start
  377.0 246.0 %all-reduce.11.cloned.1.call-done = bf16[256,2,128]{0,2,1:T(8,128)(2,1)} async-done(((bf16[256,2,128]{0,2,1:T(8,128)(2,1)}), bf16[256,2,128]{0,2,1:T(8,128)(2,1)}) %all-reduce.11.cloned.1.call-update) | async-done | bytes 131088 | tf_op jit(solution)/shard_map/psum | solution.py:56
  623.0 0.9 multiply_convert_fusion.1
  623.9 0.0 copy-done.15
  623.9 0.0 copy-done.18
  624.0 2.3 fusion.4
  626.3 1.4 fusion.1
  627.7 35.3 %psum.67 = bf16[4,4096]{1,0:T(4,128)(2,1)} all-reduce(bf16[4,4096]{1,0:T(4,128)(2,1)S(1)} %fusion.4), channel_id=1, replica_groups=mesh['slab'=32,'view'=8] {'view'}, use_global_device_ids=true, to_apply=%region_5.6 | all-reduce | flops 16384 | bytes 65536 | tf_op jit(solution)/shard_map/psum | solution.py:79
  663.0 0.0 all-reduce.13.cloned.1.call-update
  663.1 0.0 all-reduce.15.cloned.1.call-start
  663.1 2.4 fusion.19
  665.5 70.3 %all-reduce.13.cloned.1.call-done = bf16[16,4096]{1,0:T(8,128)(2,1)} async-done(((bf16[16,4096]{1,0:T(8,128)(2,1)}), bf16[16,4096]{1,0:T(8,128)(2,1)}) %all-reduce.13.cloned.1.call-update) | async-done | bytes 131088 | tf_op jit(solution)/shard_map/psum | solution.py:80
  735.8 2.3 fusion.9
  738.0 0.0 all-reduce.15.cloned.1.call-update
  738.1 0.0 all-reduce.17.cloned.1.call-start
  738.1 245.8 %all-reduce.15.cloned.1.call-done = bf16[256,2,128]{0,2,1:T(8,128)(2,1)} async-done(((bf16[256,2,128]{0,2,1:T(8,128)(2,1)}), bf16[256,2,128]{0,2,1:T(8,128)(2,1)}) %all-reduce.15.cloned.1.call-update) | async-done | bytes 131088 | tf_op jit(solution)/shard_map/psum | solution.py:56
  984.0 0.9 multiply_convert_fusion
  984.9 0.0 copy-start.5
  984.9 0.0 copy-start.8
  984.9 0.0 copy-start.9
  985.0 2.4 fusion.5
  987.4 1.4 fusion.2
  988.8 34.8 %psum.70 = bf16[4,4096]{1,0:T(4,128)(2,1)S(1)} all-reduce(bf16[4,4096]{1,0:T(4,128)(2,1)S(1)} %fusion.5), channel_id=1, replica_groups=mesh['slab'=32,'view'=8] {'view'}, use_global_device_ids=true, to_apply=%region_8.9 | all-reduce | flops 16384 | bytes 65536 | tf_op jit(solution)/shard_map/psum | solution.py:79
  1023.6 0.0 all-reduce.17.cloned.1.call-update
  1023.6 0.7 multiply_add_fusion
  1024.3 72.0 %all-reduce.17.cloned.1.call-done = bf16[16,4096]{1,0:T(8,128)(2,1)} async-done(((bf16[16,4096]{1,0:T(8,128)(2,1)}), bf16[16,4096]{1,0:T(8,128)(2,1)}) %all-reduce.17.cloned.1.call-update) | async-done | bytes 131088 | tf_op jit(solution)/shard_map/psum | solution.py:80
  1096.3 1.7 add_multiply_fusion
  (27 shorter events, 0.1 us)
Async XLA Ops:
  7.2 4.2 copy-start
  7.2 4.2 copy-start.6
  7.2 4.2 copy-start.1
  7.2 254.6 %all-reduce.7.cloned.1.call-start = ((), (), s32[]{:S(2)}) async-start(), calls=%async_computation | async-start | bytes 262144 | tf_op jit(solution)/shard_map/psum | solution.py:56
  8.3 256.9 %copy-start.14 = (bf16[2,256]{1,0:T(2,128)(2,1)}, bf16[2,256]{1,0:T(2,128)(2,1)S(1)}, u32[]{:S(2)}) copy-start(bf16[2,256]{1,0:T(2,128)(2,1)S(1)} %convert_element_type.158) | copy-start | bytes 3076
  9.1 3.7 copy-start.11
  9.1 3.8 copy-start.19
  11.4 44.5 %copy-start.20 = (f32[8,2,128]{2,1,0:T(2,128)S(1)}, f32[8,2,128]{2,1,0:T(2,128)}, u32[]{:S(2)}) copy-start(f32[8,2,128]{2,1,0:T(2,128)} %param.19) | copy-start | bytes 24580
  11.4 251.3 %copy-start.17 = (bf16[2,4,256]{2,1,0:T(4,128)(2,1)S(1)}, bf16[2,4,256]{2,1,0:T(4,128)(2,1)}, u32[]{:S(2)}) copy-start(bf16[2,4,256]{2,1,0:T(4,128)(2,1)} %param.16) | copy-start | bytes 12292
  12.8 361.9 %all-reduce.9.cloned.1.call-start = ((), (), s32[]{:S(2)}) async-start(), calls=%async_computation.1 | async-start | bytes 262144 | tf_op jit(solution)/shard_map/psum | solution.py:80
  262.8 39.2 %copy-start.4 = (f32[4,4096]{1,0:T(4,128)S(1)}, f32[4,4096]{1,0:T(4,128)}, u32[]{:S(2)}) copy-start(f32[4,4096]{1,0:T(4,128)} %param.12) | copy-start | bytes 196612
  262.8 39.2 %copy-start.7 = (f32[4,4096]{1,0:T(4,128)S(1)}, f32[4,4096]{1,0:T(4,128)}, u32[]{:S(2)}) copy-start(f32[4,4096]{1,0:T(4,128)} %param.20) | copy-start | bytes 196612
  265.1 109.5 %copy-start.2 = (f32[16,4096]{1,0:T(8,128)S(1)}, f32[16,4096]{1,0:T(8,128)}, u32[]{:S(2)}) copy-start(f32[16,4096]{1,0:T(8,128)} %param.21) | copy-start | bytes 786436
  301.9 321.0 %all-reduce.11.cloned.1.call-start = ((), (), s32[]{:S(2)}) async-start(), calls=%async_computation.2 | async-start | bytes 262144 | tf_op jit(solution)/shard_map/psum | solution.py:56
  304.3 319.7 %copy-start.15 = (bf16[2,256]{1,0:T(2,128)(2,1)S(1)}, bf16[2,256]{1,0:T(2,128)(2,1)}, u32[]{:S(2)}) copy-start(bf16[2,256]{1,0:T(2,128)(2,1)} %copy-done.14) | copy-start | bytes 3076
  304.3 319.7 %copy-start.18 = (bf16[2,4,256]{2,1,0:T(4,128)(2,1)S(1)}, bf16[2,4,256]{2,1,0:T(4,128)(2,1)}, u32[]{:S(2)}) copy-start(bf16[2,4,256]{2,1,0:T(4,128)(2,1)} %param.16) | copy-start | bytes 12292
  376.9 358.8 %all-reduce.13.cloned.1.call-start = ((), (), s32[]{:S(2)}) async-start(), calls=%async_computation.3 | async-start | bytes 262144 | tf_op jit(solution)/shard_map/psum | solution.py:80
  626.3 109.5 %copy-start.3 = (bf16[16,4096]{1,0:T(8,128)(2,1)S(1)}, bf16[16,4096]{1,0:T(8,128)(2,1)}, u32[]{:S(2)}) copy-start(bf16[16,4096]{1,0:T(8,128)(2,1)} %all-reduce.9.cloned.1.call-done) | copy-start | bytes 393220
  663.1 320.9 %all-reduce.15.cloned.1.call-start = ((), (), s32[]{:S(2)}) async-start(), calls=%async_computation.4 | async-start | bytes 262144 | tf_op jit(solution)/shard_map/psum | solution.py:56
  738.0 249.3 %copy-start.16 = (bf16[2,256]{1,0:T(2,128)(2,1)S(1)}, bf16[2,256]{1,0:T(2,128)(2,1)}, u32[]{:S(2)}) copy-start(bf16[2,256]{1,0:T(2,128)(2,1)} %copy-done.14) | copy-start | bytes 3076
  738.1 358.2 %all-reduce.17.cloned.1.call-start = ((), (), s32[]{:S(2)}) async-start(), calls=%async_computation.5 | async-start | bytes 262144 | tf_op jit(solution)/shard_map/psum | solution.py:80
  984.9 38.7 %copy-start.5 = (f32[4,4096]{1,0:T(4,128)S(1)}, f32[4,4096]{1,0:T(4,128)}, u32[]{:S(2)}) copy-start(f32[4,4096]{1,0:T(4,128)} %param.12) | copy-start | bytes 196612
  984.9 38.7 %copy-start.8 = (f32[4,4096]{1,0:T(4,128)S(1)}, f32[4,4096]{1,0:T(4,128)}, u32[]{:S(2)}) copy-start(f32[4,4096]{1,0:T(4,128)} %param.20) | copy-start | bytes 196612
  984.9 38.7 %copy-start.9 = (bf16[4,4096]{1,0:T(4,128)(2,1)S(1)}, bf16[4,4096]{1,0:T(4,128)(2,1)}, u32[]{:S(2)}) copy-start(bf16[4,4096]{1,0:T(4,128)(2,1)} %psum.64) | copy-start | bytes 98308
  984.9 38.7 %copy-start.13 = (bf16[4,4096]{1,0:T(4,128)(2,1)S(1)}, bf16[4,4096]{1,0:T(4,128)(2,1)}, u32[]{:S(2)}) copy-start(bf16[4,4096]{1,0:T(4,128)(2,1)} %psum.67) | copy-start | bytes 98308
  985.0 111.4 %copy-start.10 = (bf16[16,4096]{1,0:T(8,128)(2,1)S(1)}, bf16[16,4096]{1,0:T(8,128)(2,1)}, u32[]{:S(2)}) copy-start(bf16[16,4096]{1,0:T(8,128)(2,1)} %all-reduce.13.cloned.1.call-done) | copy-start | bytes 393220
  985.0 111.3 %copy-start.12 = (f32[4096]{0:T(1024)S(1)}, f32[4096]{0:T(1024)}, u32[]{:S(2)}) copy-start(f32[4096]{0:T(1024)} %copy-done.11) | copy-start | bytes 49156
Sparse Core Ops, SparseCore 0:
  12.9 248.8 all-reduce.6
  302.1 72.5 all-reduce.8
  377.9 245.0 all-reduce.10
  663.2 72.5 all-reduce.12
  738.8 245.0 all-reduce.14
  1023.7 72.5 all-reduce.16
where the time goes:
time: 1110 us; the launch traced here: 1100 us
  waiting for transfers between devices  873 us (79%)
  blocking collectives  186 us (17%)
  matrix products  24.1 us (2%)
  between operations  14.4 us (1%)
    psum x3, waiting for transfers between devices, body(): lax.psum((total + jnp.einsum('vzw,vzu->wvu', coarse_depth, coarse_moment,...  660 us
    psum x3, waiting for transfers between devices, body(): lax.psum(coarse_term.astype(jnp.bfloat16), 'view').astype(jnp.float32)  213 us
    psum x3, blocking collectives, body(): lax.psum(fine_term.astype(jnp.bfloat16), 'view').astype(jnp.float32)  105 us
    all_gather x1, blocking collectives, body(): lax.all_gather(measured, 'slab', axis=0, tiled=True)  42.9 us
    all_gather x1, blocking collectives, body(): lax.all_gather(ray_weight, 'slab', axis=0, tiled=True)  37.4 us
  transfers between devices with their start and end apart: 6, of which 6 were waited for; matrix products, arithmetic and copies ran while one was open for 1% of the time, Pallas kernels for 0%

commit v1 on v0

--- a/solution.py
+++ b/solution.py
@@ -1,3 +1,4 @@
+import functools
 import jax
 import jax.numpy as jnp
 from jax import lax
@@ -5,6 +6,13 @@
 
 ITERS = 3
 BLOCK = 128
+
+
+def _save_weights(original, axis_name):
+    return lax.all_gather(original, axis_name).sum(axis=0)
+
+
+direct_the_terms = functools.partial(_save_weights, axis_name="view")
 
 
 def body(
@@ -76,7 +84,7 @@
             "vzu,vxu->zx", coarse_spread, coarse_rays, preferred_element_type=jnp.float32
         )
         fine_back, coarse_back = (
-            lax.psum(fine_term.astype(jnp.bfloat16), "view").astype(jnp.float32),
+            direct_the_terms(fine_term.astype(jnp.bfloat16)).astype(jnp.float32),
             lax.psum(coarse_term.astype(jnp.bfloat16), "view").astype(jnp.float32),
         )
         fine = fine + fine_cell_weight * fine_back

time: 1110 us -> 1020 us (0.919)
  waiting for transfers between devices: 873 us -> 797 us
  blocking collectives: 186 us -> 169 us
    psum x3 -> x0, blocking collectives: 105 us -> none  [body(): lax.psum(fine_term.astype(jnp.bfloat16), 'view').astype(jnp.float32)]
    all_gather x0 -> x3, blocking collectives: none -> 88.7 us  [_save_weights(): return lax.all_gather(original, axis_name).sum(axis=0)]
    psum x3, waiting for transfers between devices: 213 us -> 137 us  [body(): lax.psum(coarse_term.astype(jnp.bfloat16), 'view').astype(jnp.float32)]
where the time goes in v1:
time: 1020 us; the launch traced here: 1010 us
  waiting for transfers between devices  797 us (78%)
  blocking collectives  169 us (17%)
  matrix products  25.2 us (2%)
  between operations  14.4 us (1%)
    psum x3, waiting for transfers between devices, body(): lax.psum((total + jnp.einsum('vzw,vzu->wvu', coarse_depth, coarse_moment,...  660 us
    psum x3, waiting for transfers between devices, body(): lax.psum(coarse_term.astype(jnp.bfloat16), 'view').astype(jnp.float32)  137 us
    all_gather x3, blocking collectives, _save_weights(): return lax.all_gather(original, axis_name).sum(axis=0)  88.7 us
    all_gather x1, blocking collectives, body(): lax.all_gather(measured, 'slab', axis=0, tiled=True)  42.9 us
    all_gather x1, blocking collectives, body(): lax.all_gather(ray_weight, 'slab', axis=0, tiled=True)  37.4 us
  transfers between devices with their start and end apart: 6, of which 6 were waited for; matrix products, arithmetic and copies ran while one was open for 1% of the time, Pallas kernels for 0%

profile of v1, /device:TPU:4, one launch (start us, length us, event | category | flops | bytes accessed | tf_op | source)
XLA Modules:
  0.0 1015.0 jit_solution(6442893837296130215)
XLA Ops:
  7.2 0.0 copy-start
  7.2 0.0 copy-start.6
  7.2 0.0 all-reduce.7.cloned.1.call-start
  7.3 0.8 convert_element_type.162
  8.1 0.1 broadcast_in_dim.10
  8.2 0.1 convert_element_type.164
  8.3 0.8 compare_reduce_fusion
  9.1 0.0 copy-start.19
  9.1 2.3 fusion.18
  11.4 0.0 copy-done
  11.4 0.0 copy-done.6
  11.4 0.0 copy-done.1
  11.4 0.0 copy-start.20
  11.4 0.0 copy-start.17
  11.4 1.3 fusion.14
  12.8 0.0 all-reduce.7.cloned.1.call-update
  12.8 0.0 all-reduce.9.cloned.1.call-start
  12.8 42.9 %all_gather.25 = f32[256,2,128]{2,1,0:T(2,128)S(1)} all-gather(f32[8,2,128]{2,1,0:T(2,128)S(1)} %copy-done.19), channel_id=1, replica_groups=mesh['slab'=32,'view'=8] {'slab'}, dimensions={0}, use_global_device_ids=true | all-gather | bytes 270336 | tf_op jit(solution)/shard_map/all_gather | solution.py:48
  55.7 0.1 copy.22
  55.9 0.0 copy-done.20
  55.9 37.4 %all_gather.24 = f32[256,2,128]{2,1,0:T(2,128)S(1)} all-gather(f32[8,2,128]{2,1,0:T(2,128)S(1)} %copy-done.20), channel_id=1, replica_groups=mesh['slab'=32,'view'=8] {'slab'}, dimensions={0}, use_global_device_ids=true | all-gather | bytes 270336 | tf_op jit(solution)/shard_map/all_gather | solution.py:49
  93.3 0.1 copy.23
  93.4 168.4 %all-reduce.7.cloned.1.call-done = bf16[256,2,128]{0,2,1:T(8,128)(2,1)} async-done(((bf16[256,2,128]{0,2,1:T(8,128)(2,1)}), bf16[256,2,128]{0,2,1:T(8,128)(2,1)}) %all-reduce.7.cloned.1.call-update) | async-done | bytes 131088 | tf_op jit(solution)/shard_map/psum | solution.py:64
  261.8 0.9 multiply_convert_fusion.2
  262.8 0.0 copy-done.17
  262.8 2.9 fusion.8
  265.7 1.4 fusion
  267.1 0.0 all-reduce.9.cloned.1.call-update
  267.2 0.0 all-reduce.11.cloned.1.call-start
  267.2 29.6 %all-gather.3 = bf16[8,4,4096]{2,1,0:T(4,128)(2,1)S(1)} all-gather(bf16[1,4,4096]{2,1,0:T(4,128)(2,1)} %fusion.8), channel_id=2, replica_groups=mesh['slab'=32,'view'=8] {'view'}, dimensions={0}, use_global_device_ids=true | all-gather | bytes 294912 | tf_op jit(solution)/shard_map/all_gather | solution.py:12
  296.8 0.7 reduce_sum.36
  297.5 2.3 fusion.20
  299.8 0.0 copy-start.18
  299.8 44.8 %all-reduce.9.cloned.1.call-done = bf16[16,4096]{1,0:T(8,128)(2,1)} async-done(((bf16[16,4096]{1,0:T(8,128)(2,1)}), bf16[16,4096]{1,0:T(8,128)(2,1)}) %all-reduce.9.cloned.1.call-update) | async-done | bytes 131088 | tf_op jit(solution)/shard_map/psum | solution.py:88
  344.7 2.2 fusion.13
  346.9 0.0 all-reduce.11.cloned.1.call-update
  347.0 0.0 all-reduce.13.cloned.1.call-start
  347.0 246.0 %all-reduce.11.cloned.1.call-done = bf16[256,2,128]{0,2,1:T(8,128)(2,1)} async-done(((bf16[256,2,128]{0,2,1:T(8,128)(2,1)}), bf16[256,2,128]{0,2,1:T(8,128)(2,1)}) %all-reduce.11.cloned.1.call-update) | async-done | bytes 131088 | tf_op jit(solution)/shard_map/psum | solution.py:64
  593.0 0.9 multiply_convert_fusion.1
  594.0 0.0 copy-done.15
  594.0 0.0 copy-done.18
  594.0 2.9 fusion.7
  596.9 1.4 fusion.1
  598.3 0.0 all-reduce.13.cloned.1.call-update
  598.3 0.0 all-reduce.15.cloned.1.call-start
  598.4 29.6 %all-gather.4 = bf16[8,4,4096]{2,1,0:T(4,128)(2,1)S(1)} all-gather(bf16[1,4,4096]{2,1,0:T(4,128)(2,1)} %fusion.7), channel_id=3, replica_groups=mesh['slab'=32,'view'=8] {'view'}, dimensions={0}, use_global_device_ids=true | all-gather | bytes 294912 | tf_op jit(solution)/shard_map/all_gather | solution.py:12
  628.0 0.7 reduce_sum.37
  628.7 2.4 fusion.22
  631.1 44.8 %all-reduce.13.cloned.1.call-done = bf16[16,4096]{1,0:T(8,128)(2,1)} async-done(((bf16[16,4096]{1,0:T(8,128)(2,1)}), bf16[16,4096]{1,0:T(8,128)(2,1)}) %all-reduce.13.cloned.1.call-update) | async-done | bytes 131088 | tf_op jit(solution)/shard_map/psum | solution.py:88
  675.9 2.3 fusion.12
  678.1 0.0 all-reduce.15.cloned.1.call-update
  678.2 0.0 all-reduce.17.cloned.1.call-start
  678.2 245.8 %all-reduce.15.cloned.1.call-done = bf16[256,2,128]{0,2,1:T(8,128)(2,1)} async-done(((bf16[256,2,128]{0,2,1:T(8,128)(2,1)}), bf16[256,2,128]{0,2,1:T(8,128)(2,1)}) %all-reduce.15.cloned.1.call-update) | async-done | bytes 131088 | tf_op jit(solution)/shard_map/psum | solution.py:64
  924.1 0.9 multiply_convert_fusion
  925.0 2.3 fusion.6
  927.4 0.0 copy-start.8
  927.4 0.0 copy-start.9
  927.4 1.4 fusion.2
  928.8 0.0 all-reduce.17.cloned.1.call-update
  928.8 29.5 %all-gather.5 = bf16[8,4,4096]{2,1,0:T(4,128)(2,1)S(1)} all-gather(bf16[1,4,4096]{2,1,0:T(4,128)(2,1)S(1)} %fusion.6), channel_id=4, replica_groups=mesh['slab'=32,'view'=8] {'view'}, dimensions={0}, use_global_device_ids=true | all-gather | bytes 294912 | tf_op jit(solution)/shard_map/all_gather | solution.py:12
  958.3 0.1 reduce_sum.38
  958.5 0.7 multiply_add_fusion
  959.1 47.2 %all-reduce.17.cloned.1.call-done = bf16[16,4096]{1,0:T(8,128)(2,1)} async-done(((bf16[16,4096]{1,0:T(8,128)(2,1)}), bf16[16,4096]{1,0:T(8,128)(2,1)}) %all-reduce.17.cloned.1.call-update) | async-done | bytes 131088 | tf_op jit(solution)/shard_map/psum | solution.py:88
  1006.4 1.7 add_multiply_fusion
  (30 shorter events, 0.1 us)
Async XLA Ops:
  7.2 4.2 copy-start
  7.2 4.2 copy-start.6
  7.2 4.2 copy-start.1
  7.2 254.6 %all-reduce.7.cloned.1.call-start = ((), (), s32[]{:S(2)}) async-start(), calls=%async_computation | async-start | bytes 262144 | tf_op jit(solution)/shard_map/psum | solution.py:64
  8.3 257.5 %copy-start.14 = (bf16[2,256]{1,0:T(2,128)(2,1)}, bf16[2,256]{1,0:T(2,128)(2,1)S(1)}, u32[]{:S(2)}) copy-start(bf16[2,256]{1,0:T(2,128)(2,1)S(1)} %convert_element_type.164) | copy-start | bytes 3076
  9.1 3.7 copy-start.11
  9.1 3.8 copy-start.19
  11.4 44.5 %copy-start.20 = (f32[8,2,128]{2,1,0:T(2,128)S(1)}, f32[8,2,128]{2,1,0:T(2,128)}, u32[]{:S(2)}) copy-start(f32[8,2,128]{2,1,0:T(2,128)} %param.19) | copy-start | bytes 24580
  11.4 251.3 %copy-start.17 = (bf16[2,4,256]{2,1,0:T(4,128)(2,1)S(1)}, bf16[2,4,256]{2,1,0:T(4,128)(2,1)}, u32[]{:S(2)}) copy-start(bf16[2,4,256]{2,1,0:T(4,128)(2,1)} %param.16) | copy-start | bytes 12292
  12.8 331.9 %all-reduce.9.cloned.1.call-start = ((), (), s32[]{:S(2)}) async-start(), calls=%async_computation.1 | async-start | bytes 262144 | tf_op jit(solution)/shard_map/psum | solution.py:88
  265.7 31.8 %copy-start.4 = (f32[4,4096]{1,0:T(4,128)S(1)}, f32[4,4096]{1,0:T(4,128)}, u32[]{:S(2)}) copy-start(f32[4,4096]{1,0:T(4,128)} %param.12) | copy-start | bytes 196612
  265.7 31.8 %copy-start.7 = (f32[4,4096]{1,0:T(4,128)S(1)}, f32[4,4096]{1,0:T(4,128)}, u32[]{:S(2)}) copy-start(f32[4,4096]{1,0:T(4,128)} %param.20) | copy-start | bytes 196612
  267.1 77.6 %copy-start.2 = (f32[16,4096]{1,0:T(8,128)S(1)}, f32[16,4096]{1,0:T(8,128)}, u32[]{:S(2)}) copy-start(f32[16,4096]{1,0:T(8,128)} %param.21) | copy-start | bytes 786436
  267.2 325.9 %all-reduce.11.cloned.1.call-start = ((), (), s32[]{:S(2)}) async-start(), calls=%async_computation.2 | async-start | bytes 262144 | tf_op jit(solution)/shard_map/psum | solution.py:64
  299.8 294.2 %copy-start.15 = (bf16[2,256]{1,0:T(2,128)(2,1)S(1)}, bf16[2,256]{1,0:T(2,128)(2,1)}, u32[]{:S(2)}) copy-start(bf16[2,256]{1,0:T(2,128)(2,1)} %copy-done.14) | copy-start | bytes 3076
  299.8 294.2 %copy-start.18 = (bf16[2,4,256]{2,1,0:T(4,128)(2,1)S(1)}, bf16[2,4,256]{2,1,0:T(4,128)(2,1)}, u32[]{:S(2)}) copy-start(bf16[2,4,256]{2,1,0:T(4,128)(2,1)} %param.16) | copy-start | bytes 12292
  347.0 328.9 %all-reduce.13.cloned.1.call-start = ((), (), s32[]{:S(2)}) async-start(), calls=%async_computation.3 | async-start | bytes 262144 | tf_op jit(solution)/shard_map/psum | solution.py:88
  598.3 77.6 %copy-start.3 = (bf16[16,4096]{1,0:T(8,128)(2,1)S(1)}, bf16[16,4096]{1,0:T(8,128)(2,1)}, u32[]{:S(2)}) copy-start(bf16[16,4096]{1,0:T(8,128)(2,1)} %all-reduce.9.cloned.1.call-done) | copy-start | bytes 393220
  598.3 325.7 %all-reduce.15.cloned.1.call-start = ((), (), s32[]{:S(2)}) async-start(), calls=%async_computation.4 | async-start | bytes 262144 | tf_op jit(solution)/shard_map/psum | solution.py:64
  678.2 328.2 %all-reduce.17.cloned.1.call-start = ((), (), s32[]{:S(2)}) async-start(), calls=%async_computation.5 | async-start | bytes 262144 | tf_op jit(solution)/shard_map/psum | solution.py:88
  925.0 2.3 copy-start.16
  927.4 31.1 %copy-start.5 = (f32[4,4096]{1,0:T(4,128)S(1)}, f32[4,4096]{1,0:T(4,128)}, u32[]{:S(2)}) copy-start(f32[4,4096]{1,0:T(4,128)} %param.12) | copy-start | bytes 196612
  927.4 31.1 %copy-start.8 = (f32[4,4096]{1,0:T(4,128)S(1)}, f32[4,4096]{1,0:T(4,128)}, u32[]{:S(2)}) copy-start(f32[4,4096]{1,0:T(4,128)} %param.20) | copy-start | bytes 196612
  927.4 31.1 %copy-start.9 = (bf16[4,4096]{1,0:T(4,128)(2,1)S(1)}, bf16[4,4096]{1,0:T(4,128)(2,1)}, u32[]{:S(2)}) copy-start(bf16[4,4096]{1,0:T(4,128)(2,1)} %reduce_sum.36) | copy-start | bytes 98308
  927.4 31.1 %copy-start.13 = (bf16[4,4096]{1,0:T(4,128)(2,1)S(1)}, bf16[4,4096]{1,0:T(4,128)(2,1)}, u32[]{:S(2)}) copy-start(bf16[4,4096]{1,0:T(4,128)(2,1)} %reduce_sum.37) | copy-start | bytes 98308
  927.4 79.0 %copy-start.10 = (bf16[16,4096]{1,0:T(8,128)(2,1)S(1)}, bf16[16,4096]{1,0:T(8,128)(2,1)}, u32[]{:S(2)}) copy-start(bf16[16,4096]{1,0:T(8,128)(2,1)} %all-reduce.13.cloned.1.call-done) | copy-start | bytes 393220
  927.4 79.0 %copy-start.12 = (f32[4096]{0:T(1024)S(1)}, f32[4096]{0:T(1024)}, u32[]{:S(2)}) copy-start(f32[4096]{0:T(1024)} %copy-done.11) | copy-start | bytes 49156
Sparse Core Ops, SparseCore 0:
  12.9 248.8 all-reduce.6
  267.3 77.3 all-reduce.8
  347.9 245.0 all-reduce.10
  598.5 77.3 all-reduce.12
  678.9 245.0 all-reduce.14
  929.0 77.3 all-reduce.16
